TPU v7x, 512 devices: a whole 4x4x16 slice. The times are simulated.
512 devices in a mesh: cell: 32 (over z_lo, x, core), feat: 16 (over z_hi, y).
Axes of the slice: x: 4, y: 4, z: 16 (z_hi: 4, z_lo: 4; z = z_hi * 4 + z_lo), core: 2. Of those that a mesh axis runs over, the one named last changes fastest.
Arguments:
- rna_counts: bfloat16 [65536, 4096], P('cell', 'feat'), may hold values from -6 to 6
- rna_embed: bfloat16 [65536, 64], P('cell'), may hold values from -3 to 3
- rna_potential: float32 [65536], P('cell'), may hold values from -1 to 1
- atac_counts: bfloat16 [16384, 16384], P('feat', 'cell'), may hold values from -6 to 6
- atac_embed: bfloat16 [16384, 64], P('feat'), may hold values from -3 to 3
- atac_potential: bfloat16 [16384], P('feat'), may hold values from -1 to 1
- panel_ids: int32 [1024], P('feat'), may hold values from 0 to 16383, as said below
Outputs:
- feature_cross: bfloat16 [4096, 16384], P('feat', 'cell')
- gene_term: float32 [4096], P('feat')
- peak_term: float32 [16384], P('cell')
Inputs may be any that keep to these rules, and one draw needn't show every extreme that they name: `panel_ids`: the ids in slots k * 64 to (k + 1) * 64 - 1 are distinct and lie among ATAC cells k * 1024 to (k + 1) * 1024 - 1.
All inputs are finite; a program needn't handle non-finite values.
Results may differ from a plain program's by a relative error of at most 0.0058.
Values may be sent and summed in bfloat16 or wider, within the bound.
A program may use at most 64 MiB of HBM per device.

v0:
```python
import math

import jax
import jax.numpy as jnp
from jax import lax
from jax.sharding import PartitionSpec as P


def local(rna_counts, rna_embed, rna_potential, atac_counts, atac_embed, atac_potential, panel_ids):
    owner = lax.axis_index("feat")
    local_ids = panel_ids - owner * atac_counts.shape[0]
    chosen_rows = jnp.take(atac_counts, local_ids, axis=0)
    chosen_embed = jnp.take(atac_embed, local_ids, axis=0)
    chosen_potential = jnp.take(atac_potential, local_ids, axis=0)
    panel_rows, panel_embed, panel_potential = (
        lax.all_gather(chosen_rows, "feat", axis=0, tiled=True),
        lax.all_gather(chosen_embed, "feat", axis=0, tiled=True),
        lax.all_gather(chosen_potential, "feat", axis=0, tiled=True),
    )
    panel_float = panel_potential.astype(jnp.float32)
    inverse = 1.0 / math.sqrt(rna_embed.shape[1])
    rows_here = rna_counts.shape[0]
    genes_here = rna_counts.shape[1]
    panel_size = panel_embed.shape[0]
    height = min(512, rows_here)
    number = rows_here // height
    items = (
        rna_counts.reshape(number, height, genes_here),
        rna_embed.reshape(number, height, rna_embed.shape[1]),
        rna_potential.reshape(number, height),
    )

    def advance(carry, item):
        total, gene_sum, panel_mass = carry
        block_rows, block_embed, block_potential = item
        score = lax.dot_general(
            block_embed, panel_embed, (((1,), (1,)), ((), ())), preferred_element_type=jnp.float32
        )
        coupling = jnp.exp(
            block_potential[:, None] + panel_float[None, :] + score * inverse
        ).astype(jnp.bfloat16)
        widened = coupling.astype(jnp.float32)
        row_mass = jnp.sum(widened, axis=1)
        panel_mass = panel_mass + jnp.sum(widened, axis=0)
        total = total + lax.dot_general(
            block_rows, coupling, (((0,), (0,)), ((), ())), preferred_element_type=jnp.float32
        )
        squares = jnp.square(block_rows.astype(jnp.float32))
        gene_sum = gene_sum + jnp.dot(row_mass, squares, precision=lax.Precision.HIGHEST)
        return ((total, gene_sum, panel_mass), None)

    start = (
        jnp.zeros((genes_here, panel_size), jnp.float32),
        jnp.zeros((genes_here,), jnp.float32),
        jnp.zeros((panel_size,), jnp.float32),
    )
    (total, gene_sum, panel_mass), unused = lax.scan(advance, start, items)
    total, gene_sum, panel_mass = lax.psum((total, gene_sum, panel_mass), "cell")
    reduced = total.astype(jnp.bfloat16)
    all_rows = rows_here * lax.axis_size("cell")
    scale = 1.0 / math.sqrt(all_rows * panel_size)
    mass_scale = 1.0 / (all_rows * panel_size)
    feature_cross = (
        jnp.dot(reduced, panel_rows, preferred_element_type=jnp.float32) * scale
    ).astype(jnp.bfloat16)
    gene_term = gene_sum * mass_scale
    peak_term = (
        jnp.dot(
            panel_mass, jnp.square(panel_rows.astype(jnp.float32)), precision=lax.Precision.HIGHEST
        )
        * mass_scale
    )
    return (feature_cross, gene_term, peak_term)


def solution(mesh):
    placed = (
        P("cell", "feat"),
        P("cell", None),
        P("cell"),
        P("feat", "cell"),
        P("feat", None),
        P("feat"),
        P("feat"),
    )
    return jax.shard_map(
        local,
        mesh=mesh,
        in_specs=placed,
        out_specs=(P("feat", "cell"), P("feat"), P("cell")),
        check_vma=False,
    )
```

profile of v0, /device:TPU:1, one launch (start us, length us, event | category | flops | bytes accessed | tf_op | source)
XLA Modules:
  0.0 294.4 jit_solution(12561693052006271583)
XLA Ops:
  7.2 0.0 all-gather.2.cloned.1.call-start
  7.3 0.7 compare_and_fusion
  8.0 0.4 copy-done
  8.4 0.7 gather_fusion.2
  9.1 0.7 broadcast_select_fusion
  9.9 0.8 gather_fusion
  10.7 1.3 dynamic-slice
  12.6 0.2 dynamic-update-slice
  12.9 53.3 %all-reduce = bf16[1024]{0:T(1024)(128)(2,1)S(1)} all-reduce(bf16[1024]{0:T(1024)(128)(2,1)S(1)} %dynamic-update-slice), channel_id=1, replica_groups=mesh['cell'=32,'feat'=16] {'feat'}, use_global_device_ids=true, to_apply=%add | all-reduce | flops 1024 | bytes 4096
  66.2 0.2 copy.13
  66.4 0.6 gather_fusion.1
  67.0 0.1 broadcast_select_fusion.1
  67.1 48.7 %all_gather.10 = bf16[1024,64]{1,0:T(8,128)(2,1)S(1)} all-gather(bf16[64,64]{1,0:T(8,128)(2,1)S(1)} %broadcast_select_fusion.1), channel_id=1, replica_groups=mesh['cell'=32,'feat'=16] {'feat'}, dimensions={0}, use_global_device_ids=true | all-gather | bytes 139264 | tf_op jit(solution)/shard_map/all_gather | solution.py:17
  115.8 1.0 copy.12
  116.8 18.1 %while.15 = (s32[]{:T(128)}, f32[256,1024]{1,0:T(8,128)S(1)}, f32[256]{0:T(256)S(1)}, f32[1024]{0:T(1024)S(1)}, bf16[4,512,256]{2,1,0:T(8,128)(2,1)}, /*index=5*...) while((s32[]{:T(128)}, f32[256,1024]{1,0:T(8,128)S(1)}, ...), condition=%wide.region_3.4_spmd.clone, body=%wide.region_0.3_spmd.clone.sunk | while | flops 341574656 | bytes 5017213 | solution.py:57
  116.8 1.7 convert_reduce_fusion.3
  118.5 1.5 convolution_add_fusion.2
  120.0 1.3 fusion.34
  121.3 1.7 convert_reduce_fusion.3
  123.0 1.5 convolution_add_fusion.2
  124.5 1.3 fusion.34
  125.9 1.7 convert_reduce_fusion.3
  127.5 1.5 convolution_add_fusion.2
  129.0 1.3 fusion.34
  130.4 1.7 convert_reduce_fusion.3
  132.1 1.5 convolution_add_fusion.2
  133.6 1.3 fusion.34
  134.9 147.8 %all-reduce.3 = (bf16[256,1024]{1,0:T(8,128)(2,1)S(1)}, f32[256]{0:T(256)S(1)}, f32[1024]{0:T(1024)S(1)}) all-reduce(f32[256,1024]{1,0:T(8,128)S(1)} %get-tuple-element.52, f32[256]{0:T(256)S(1)} %get-tuple-element.53, f32[1024]{0:T(1024)S(1)} %get-tuple-element.54), channel_id=1, replica_groups=mesh['cell'=32,'feat'=16] {'cell'}, use_global_device_ids=true, to_apply=%region_4.5 | all-reduce | flops 263424 | bytes 1583104 | tf_op jit(solution)/shard_map/psum | solution.py:58
  282.7 0.6 broadcast_multiply_fusion.1
  283.3 2.5 fusion.12
  285.8 0.6 broadcast_multiply_fusion
  286.4 1.1 fusion.15
  (33 shorter events, 0.3 us)
Async XLA Ops:
  7.2 1.2 copy-start
  7.2 2.7 copy-start.1
  7.2 59.0 %copy-start.4 = (bf16[1024,64]{0,1:T(8,128)(2,1)S(1)}, bf16[1024,64]{0,1:T(8,128)(2,1)}, u32[]{:S(2)}) copy-start(bf16[1024,64]{0,1:T(8,128)(2,1)} %param.13) | copy-start | bytes 393220
  7.2 276.1 %all-gather.2.cloned.1.call-start = ((), (), s32[]{:S(2)}) async-start(), calls=%async_computation | async-start | bytes 1114112 | tf_op jit(solution)/shard_map/all_gather | solution.py:16
  8.4 107.3 %copy-start.3 = (bf16[2048,64]{0,1:T(8,128)(2,1)S(1)}, bf16[2048,64]{0,1:T(8,128)(2,1)}, u32[]{:S(2)}) copy-start(bf16[2048,64]{0,1:T(8,128)(2,1)} %param.10) | copy-start | bytes 786436
  9.9 106.9 %copy-start.5 = (f32[2048]{0:T(1024)S(1)}, f32[2048]{0:T(1024)}, u32[]{:S(2)}) copy-start(f32[2048]{0:T(1024)} %param.11) | copy-start | bytes 24580
  283.3 3.1 %copy-start.2 = (bf16[1024,512]{1,0:T(8,128)(2,1)S(1)}, bf16[1024,512]{1,0:T(8,128)(2,1)}, u32[]{:S(2)}) copy-start(bf16[1024,512]{1,0:T(8,128)(2,1)} %all-gather.2.cloned.1.call-done) | copy-start | bytes 3145732
Sparse Core Ops, SparseCore 0:
  11.6 83.7 all-gather.1
where the time goes:
time: 299 us; the launch traced here: 294 us
  blocking collectives  250 us (84%)
  matrix products  21.4 us (7%)
  between operations  14.8 us (5%)
  local copies, waits for them, and re-layouts  5.31 us (2%)
    psum x1, blocking collectives, local(): lax.psum((total, gene_sum, panel_mass), 'cell')  148 us
    unnamed x1, blocking collectives  53.3 us
    all_gather x1, blocking collectives, local(): lax.all_gather(chosen_embed, 'feat', axis=0, tiled=True)  48.7 us
    dot_general x4, matrix products, advance(): lax.dot_general(block_embed, panel_embed, (((1,), (1,)), ((), ())), prefe...  6.7 us
  transfers between devices with their start and end apart: 1, of which 0 were waited for; matrix products, arithmetic and copies ran while one was open for 8% of the time, Pallas kernels for 0%

commit v1 on v0

--- a/solution.py
+++ b/solution.py
@@ -3,21 +3,58 @@
 import jax
 import jax.numpy as jnp
 from jax import lax
+from jax.sharding import Mesh
 from jax.sharding import PartitionSpec as P
+
+CELL = ("z_lo", "x", "core")
+FEAT = ("z_hi", "y")
+SIZES = {"z_lo": 4, "x": 4, "core": 2, "z_hi": 4, "y": 4}
+HALVING = (("core", 1), ("x", 1), ("z_lo", 1), ("x", 2), ("z_lo", 2))
+
+
+def _half(piece, axis, bit):
+    h = piece.shape[0] // 2
+    upper = ((lax.axis_index(axis) & bit) != 0).astype(jnp.int32)
+    keep = lax.dynamic_slice_in_dim(piece, upper * h, h, axis=0)
+    send = lax.dynamic_slice_in_dim(piece, (1 - upper) * h, h, axis=0)
+    return keep, send
+
+
+def _swap(value, axis, bit):
+    return lax.ppermute(value, axis, [(i, i ^ bit) for i in range(SIZES[axis])])
+
+
+def _join(piece, got, axis, bit):
+    lower = (lax.axis_index(axis) & bit) == 0
+    return jnp.where(lower, jnp.concatenate([piece, got]), jnp.concatenate([got, piece]))
+
+
+def cell_sum(total, masses):
+    for axis, bit in HALVING:
+        keep_t, send_t = _half(total, axis, bit)
+        keep_m, send_m = _half(masses, axis, bit)
+        got_t, got_m = _swap((send_t, send_m), axis, bit)
+        total, masses = keep_t + got_t, keep_m + got_m
+    reduced = total.astype(jnp.bfloat16)
+    for axis, bit in reversed(HALVING):
+        got_t, got_m = _swap((reduced, masses), axis, bit)
+        reduced = _join(reduced, got_t, axis, bit)
+        masses = _join(masses, got_m, axis, bit)
+    return reduced, masses
 
 
 def local(rna_counts, rna_embed, rna_potential, atac_counts, atac_embed, atac_potential, panel_ids):
-    owner = lax.axis_index("feat")
+    owner = lax.axis_index(FEAT)
     local_ids = panel_ids - owner * atac_counts.shape[0]
     chosen_rows = jnp.take(atac_counts, local_ids, axis=0)
     chosen_embed = jnp.take(atac_embed, local_ids, axis=0)
     chosen_potential = jnp.take(atac_potential, local_ids, axis=0)
-    panel_rows, panel_embed, panel_potential = (
-        lax.all_gather(chosen_rows, "feat", axis=0, tiled=True),
-        lax.all_gather(chosen_embed, "feat", axis=0, tiled=True),
-        lax.all_gather(chosen_potential, "feat", axis=0, tiled=True),
-    )
-    panel_float = panel_potential.astype(jnp.float32)
+    small = jnp.concatenate([chosen_embed, chosen_potential[:, None]], axis=1)
+    small = lax.all_gather(small, "y", axis=0, tiled=True)
+    small = lax.all_gather(small, "z_hi", axis=0, tiled=True)
+    panel_embed = small[:, :-1]
+    panel_float = small[:, -1].astype(jnp.float32)
+    panel_rows = lax.all_gather(chosen_rows, FEAT, axis=0, tiled=True)
     inverse = 1.0 / math.sqrt(rna_embed.shape[1])
     rows_here = rna_counts.shape[0]
     genes_here = rna_counts.shape[1]
@@ -55,9 +92,10 @@
         jnp.zeros((panel_size,), jnp.float32),
     )
     (total, gene_sum, panel_mass), unused = lax.scan(advance, start, items)
-    total, gene_sum, panel_mass = lax.psum((total, gene_sum, panel_mass), "cell")
-    reduced = total.astype(jnp.bfloat16)
-    all_rows = rows_here * lax.axis_size("cell")
+    reduced, masses = cell_sum(total, jnp.concatenate([gene_sum, panel_mass]))
+    gene_sum = masses[:genes_here]
+    panel_mass = masses[genes_here:]
+    all_rows = rows_here * lax.axis_size(CELL)
     scale = 1.0 / math.sqrt(all_rows * panel_size)
     mass_scale = 1.0 / (all_rows * panel_size)
     feature_cross = (
@@ -74,19 +112,20 @@
 
 
 def solution(mesh):
+    split = Mesh(mesh.devices.reshape(4, 4, 2, 4, 4), CELL + FEAT)
     placed = (
-        P("cell", "feat"),
-        P("cell", None),
-        P("cell"),
-        P("feat", "cell"),
-        P("feat", None),
-        P("feat"),
-        P("feat"),
+        P(CELL, FEAT),
+        P(CELL, None),
+        P(CELL),
+        P(FEAT, CELL),
+        P(FEAT, None),
+        P(FEAT),
+        P(FEAT),
     )
     return jax.shard_map(
         local,
-        mesh=mesh,
+        mesh=split,
         in_specs=placed,
-        out_specs=(P("feat", "cell"), P("feat"), P("cell")),
+        out_specs=(P(FEAT, CELL), P(FEAT), P(CELL)),
         check_vma=False,
     )

time: 299 us -> 170 us (0.57); the launches traced: 294 us -> 168 us
  blocking collectives: 250 us -> 35.6 us
  starting transfers between devices: 0.04 us -> 73 us
  waiting for transfers between devices: 0.02 us -> 13.9 us
    psum x1 -> x0, blocking collectives: 148 us -> none  [local(): lax.psum((total, gene_sum, panel_mass), 'cell')]
    ppermute x0 -> x20, starting transfers between devices: none -> 72.9 us  [_swap(): return lax.ppermute(value, axis, [(i, i ^ bit) for i in range(SIZES[axis])])]
    unnamed x1 -> x0, blocking collectives: 53.3 us -> none
    ppermute x0 -> x20, waiting for transfers between devices: none -> 13.9 us  [_swap(): return lax.ppermute(value, axis, [(i, i ^ bit) for i in range(SIZES[axis])])]
    all_gather x1 -> x2, blocking collectives: 48.7 us -> 35.6 us  [the longest x1 25.3 us: local(): small = lax.all_gather(small, 'z_hi', axis=0, tiled=True)]
  transfers between devices with their start and end apart: 1 -> 21, of which waited for: 0 -> 7; matrix products, arithmetic and copies ran while one was open for 8% -> 4% of each run, Pallas kernels for 0% -> 0%
where the time goes in v1:
time: 170 us; the launch traced here: 168 us
  starting transfers between devices  73 us (43%)
  blocking collectives  35.6 us (21%)
  matrix products  21.4 us (13%)
  between operations  14.6 us (9%)
  waiting for transfers between devices  13.9 us (8%)
  local copies, waits for them, and re-layouts  5.62 us (3%)
  other arithmetic  4.18 us (2%)
    ppermute x20, starting transfers between devices, _swap(): return lax.ppermute(value, axis, [(i, i ^ bit) for i in range(SIZES[axis])])  72.9 us
    all_gather x1, blocking collectives, local(): small = lax.all_gather(small, 'z_hi', axis=0, tiled=True)  25.3 us
    ppermute x20, waiting for transfers between devices, _swap(): return lax.ppermute(value, axis, [(i, i ^ bit) for i in range(SIZES[axis])])  13.9 us
    all_gather x1, blocking collectives, local(): small = lax.all_gather(small, 'y', axis=0, tiled=True)  10.3 us
    dot_general x4, matrix products, advance(): lax.dot_general(block_embed, panel_embed, (((1,), (1,)), ((), ())), prefe...  6.7 us
    dot_general x4, matrix products, advance(): lax.dot_general(block_rows, coupling, (((0,), (0,)), ((), ())), preferred...  5.96 us
    dot_general x4, matrix products, advance(): jnp.dot(row_mass, squares, precision=lax.Precision.HIGHEST)  5.05 us
  transfers between devices with their start and end apart: 21, of which 7 were waited for; matrix products, arithmetic and copies ran while one was open for 4% of the time, Pallas kernels for 0%

profile of v1, /device:TPU:1, one launch (start us, length us, event | category | flops | bytes accessed | tf_op | source)
XLA Modules:
  0.0 168.4 jit_solution(1563563666693816153)
XLA Ops:
  11.5 10.3 %all_gather.9 = bf16[256,65]{1,0:T(8,128)(2,1)S(1)} all-gather(bf16[64,65]{1,0:T(8,128)(2,1)S(1)} %pad_maximum_fusion), channel_id=1, replica_groups=mesh['z_lo'=4,'x'=4,'core'=2,'z_hi'=4,'y'=4] {'y'}, dimensions={0}, use_global_device_ids=true | all-gather | bytes 41600 | tf_op jit(solution)/shard_map/all_gather | solution.py:53
  21.8 25.3 %all_gather.10 = bf16[1024,65]{1,0:T(8,128)(2,1)S(1)} all-gather(bf16[256,65]{1,0:T(8,128)(2,1)S(1)} %all_gather.9), channel_id=1, replica_groups=mesh['z_lo'=4,'x'=4,'core'=2,'z_hi'=4,'y'=4] {'z_hi'}, dimensions={0}, use_global_device_ids=true | all-gather | bytes 166400 | tf_op jit(solution)/shard_map/all_gather | solution.py:54
  48.4 18.1 %while.15 = (s32[]{:T(128)}, f32[256,1024]{1,0:T(8,128)S(1)}, f32[256]{0:T(256)S(1)}, f32[1024]{0:T(1024)S(1)}, bf16[4,512,256]{2,1,0:T(8,128)(2,1)}, /*index=5*...) while((s32[]{:T(128)}, f32[256,1024]{1,0:T(8,128)S(1)}, ...), condition=%wide.region_3.4_spmd.clone, body=%wide.region_0.3_spmd.clone.sunk | while | flops 341574656 | bytes 5017213 | solution.py:94
  48.4 1.7 convert_reduce_fusion.4
  53.0 1.7 convert_reduce_fusion.4
  54.6 1.5 convolution_add_fusion.2
  57.5 1.7 convert_reduce_fusion.4
  62.0 1.7 convert_reduce_fusion.4
  66.7 8.7 %collective-permute-start.10 = (f32[640]{0:T(1024)S(1)}, f32[640]{0:T(1024)S(1)}, u32[]{:S(2)}, u32[]{:S(2)}) collective-permute-start(f32[640]{0:T(1024)S(1)} %dynamic_slice.83), channel_id=1, source_target_pairs={{0,16},{16,0},{1,17},{17,1},{2,18},{18,2},{3,19},{19,3},{4,20},{20... | collective-permute-start | bytes 7688 | tf_op jit(solution)/shard_map/ppermute | solution.py:24
  75.5 1.9 %collective-permute-start = (f32[128,1024]{1,0:T(8,128)S(1)}, f32[128,1024]{1,0:T(8,128)S(1)}, u32[]{:S(2)}, u32[]{:S(2)}) collective-permute-start(f32[128,1024]{1,0:T(8,128)S(1)} %constant_dynamic-slice_fusion.5), channel_id=1, source_target_pairs={{0,16},{16,0},{1,17},{17,1},{2,18},{18,2},{3,19},{19,3},{4,20},{20... | collective-permute-start | bytes 1572872 | tf_op jit(solution)/shard_map/ppermute | solution.py:24
  79.0 3.1 %collective-permute-start.11 = (f32[320]{0:T(512)S(1)}, f32[320]{0:T(512)S(1)}, u32[]{:S(2)}, u32[]{:S(2)}) collective-permute-start(f32[320]{0:T(512)S(1)} %dynamic_slice.85), channel_id=1, source_target_pairs={{0,32},{32,0},{64,96},{96,64},{1,33},{33,1},{65,97},{97,65},{2,34}... | collective-permute-start | bytes 3848 | tf_op jit(solution)/shard_map/ppermute | solution.py:24
  83.5 2.1 %collective-permute-start.12 = (f32[160]{0:T(256)S(1)}, f32[160]{0:T(256)S(1)}, u32[]{:S(2)}, u32[]{:S(2)}) collective-permute-start(f32[160]{0:T(256)S(1)} %dynamic_slice.87), channel_id=1, source_target_pairs={{0,128},{128,0},{256,384},{384,256},{1,129},{129,1},{257,385},{385... | collective-permute-start | bytes 1928 | tf_op jit(solution)/shard_map/ppermute | solution.py:24
  85.7 3.1 %collective-permute-start.1 = (f32[64,1024]{1,0:T(8,128)S(1)}, f32[64,1024]{1,0:T(8,128)S(1)}, u32[]{:S(2)}, u32[]{:S(2)}) collective-permute-start(f32[64,1024]{1,0:T(8,128)S(1)} %constant_dynamic-slice_fusion.4), channel_id=1, source_target_pairs={{0,32},{32,0},{64,96},{96,64},{1,33},{33,1},{65,97},{97,65},{2,34}... | collective-permute-start | bytes 786440 | tf_op jit(solution)/shard_map/ppermute | solution.py:24
  89.0 4.3 %collective-permute-start.13 = (f32[80]{0:T(128)S(1)}, f32[80]{0:T(128)S(1)}, u32[]{:S(2)}, u32[]{:S(2)}) collective-permute-start(f32[80]{0:T(128)S(1)} %dynamic_slice.89), channel_id=1, source_target_pairs={{0,64},{32,96},{64,0},{96,32},{1,65},{33,97},{65,1},{97,33},{2,66}... | collective-permute-start | bytes 968 | tf_op jit(solution)/shard_map/ppermute | solution.py:24
  93.4 2.1 %collective-permute-done.13 = f32[80]{0:T(128)S(1)} collective-permute-done((f32[80]{0:T(128)S(1)}, f32[80]{0:T(128)S(1)}, u32[]{:S(2)}, u32[]{:S(2)}) %collective-permute-start.13) | collective-permute-done | bytes 352 | tf_op jit(solution)/shard_map/ppermute | solution.py:24
  95.6 3.5 %collective-permute-start.14 = (f32[40]{0:T(128)S(1)}, f32[40]{0:T(128)S(1)}, u32[]{:S(2)}, u32[]{:S(2)}) collective-permute-start(f32[40]{0:T(128)S(1)} %dynamic_slice.91), channel_id=1, source_target_pairs={{0,256},{128,384},{256,0},{384,128},{1,257},{129,385},{257,1},{385... | collective-permute-start | bytes 488 | tf_op jit(solution)/shard_map/ppermute | solution.py:24
  99.2 2.1 %collective-permute-start.2 = (f32[32,1024]{1,0:T(8,128)S(1)}, f32[32,1024]{1,0:T(8,128)S(1)}, u32[]{:S(2)}, u32[]{:S(2)}) collective-permute-start(f32[32,1024]{1,0:T(8,128)S(1)} %constant_dynamic-slice_fusion.3), channel_id=1, source_target_pairs={{0,128},{128,0},{256,384},{384,256},{1,129},{129,1},{257,385},{385... | collective-permute-start | bytes 393224 | tf_op jit(solution)/shard_map/ppermute | solution.py:24
  101.4 3.7 %collective-permute-start.15 = (f32[40]{0:T(128)S(1)}, f32[40]{0:T(128)S(1)}, u32[]{:S(2)}, u32[]{:S(2)}) collective-permute-start(f32[40]{0:T(128)S(1)} %dynamic-slice_add_fusion.7), channel_id=1, source_target_pairs={{0,256},{128,384},{256,0},{384,128},{1,257},{129,385},{257,1},{385... | collective-permute-start | bytes 488 | tf_op jit(solution)/shard_map/ppermute | solution.py:24
  105.9 3.9 %collective-permute-start.3 = (f32[16,1024]{1,0:T(8,128)S(1)}, f32[16,1024]{1,0:T(8,128)S(1)}, u32[]{:S(2)}, u32[]{:S(2)}) collective-permute-start(f32[16,1024]{1,0:T(8,128)S(1)} %constant_dynamic-slice_fusion.2), channel_id=1, source_target_pairs={{0,64},{32,96},{64,0},{96,32},{1,65},{33,97},{65,1},{97,33},{2,66}... | collective-permute-start | bytes 196616 | tf_op jit(solution)/shard_map/ppermute | solution.py:24
  109.8 2.9 %collective-permute-start.16 = (f32[80]{0:T(128)S(1)}, f32[80]{0:T(128)S(1)}, u32[]{:S(2)}, u32[]{:S(2)}) collective-permute-start(f32[80]{0:T(128)S(1)} %broadcast_select_fusion.2), channel_id=1, source_target_pairs={{0,64},{32,96},{64,0},{96,32},{1,65},{33,97},{65,1},{97,33},{2,66}... | collective-permute-start | bytes 968 | tf_op jit(solution)/shard_map/ppermute | solution.py:24
  112.8 2.3 %collective-permute-start.4 = (f32[8,1024]{1,0:T(8,128)S(1)}, f32[8,1024]{1,0:T(8,128)S(1)}, u32[]{:S(2)}, u32[]{:S(2)}) collective-permute-start(f32[8,1024]{1,0:T(8,128)S(1)} %constant_dynamic-slice_fusion.1), channel_id=1, source_target_pairs={{0,256},{128,384},{256,0},{384,128},{1,257},{129,385},{257,1},{385... | collective-permute-start | bytes 98312 | tf_op jit(solution)/shard_map/ppermute | solution.py:24
  115.7 2.9 %collective-permute-start.17 = (f32[160]{0:T(256)S(1)}, f32[160]{0:T(256)S(1)}, u32[]{:S(2)}, u32[]{:S(2)}) collective-permute-start(f32[160]{0:T(256)S(1)} %maximum_select_fusion.9), channel_id=1, source_target_pairs={{0,128},{128,0},{256,384},{384,256},{1,129},{129,1},{257,385},{385... | collective-permute-start | bytes 1928 | tf_op jit(solution)/shard_map/ppermute | solution.py:24
  118.7 3.1 %collective-permute-start.5 = (bf16[8,1024]{1,0:T(8,128)(2,1)S(1)}, bf16[8,1024]{1,0:T(8,128)(2,1)S(1)}, u32[]{:S(2)}, u32[]{:S(2)}) collective-permute-start(bf16[8,1024]{1,0:T(8,128)(2,1)S(1)} %add_convert_fusion), channel_id=1, source_target_pairs={{0,256},{128,384},{256,0},{384,128},{1,257},{129,385},{257,1},{385... | collective-permute-start | bytes 49160 | tf_op jit(solution)/shard_map/ppermute | solution.py:24
  121.9 1.9 %collective-permute-start.18 = (f32[320]{0:T(512)S(1)}, f32[320]{0:T(512)S(1)}, u32[]{:S(2)}, u32[]{:S(2)}) collective-permute-start(f32[320]{0:T(512)S(1)} %maximum_select_fusion.8), channel_id=1, source_target_pairs={{0,32},{32,0},{64,96},{96,64},{1,33},{33,1},{65,97},{97,65},{2,34}... | collective-permute-start | bytes 3848 | tf_op jit(solution)/shard_map/ppermute | solution.py:24
  124.2 4.2 %collective-permute-start.6 = (bf16[16,1024]{1,0:T(8,128)(2,1)S(1)}, bf16[16,1024]{1,0:T(8,128)(2,1)S(1)}, u32[]{:S(2)}, u32[]{:S(2)}) collective-permute-start(bf16[16,1024]{1,0:T(8,128)(2,1)S(1)} %maximum_select_fusion.5), channel_id=1, source_target_pairs={{0,64},{32,96},{64,0},{96,32},{1,65},{33,97},{65,1},{97,33},{2,66}... | collective-permute-start | bytes 98312 | tf_op jit(solution)/shard_map/ppermute | solution.py:24
  128.5 10.6 %collective-permute-start.19 = (f32[640]{0:T(1024)S(1)}, f32[640]{0:T(1024)S(1)}, u32[]{:S(2)}, u32[]{:S(2)}) collective-permute-start(f32[640]{0:T(1024)S(1)} %maximum_select_fusion.7), channel_id=1, source_target_pairs={{0,16},{16,0},{1,17},{17,1},{2,18},{18,2},{3,19},{19,3},{4,20},{20... | collective-permute-start | bytes 7688 | tf_op jit(solution)/shard_map/ppermute | solution.py:24
  139.2 3.2 %collective-permute-start.7 = (bf16[32,1024]{1,0:T(8,128)(2,1)S(1)}, bf16[32,1024]{1,0:T(8,128)(2,1)S(1)}, u32[]{:S(2)}, u32[]{:S(2)}) collective-permute-start(bf16[32,1024]{1,0:T(8,128)(2,1)S(1)} %maximum_select_fusion.4), channel_id=1, source_target_pairs={{0,128},{128,0},{256,384},{384,256},{1,129},{129,1},{257,385},{385... | collective-permute-start | bytes 196616 | tf_op jit(solution)/shard_map/ppermute | solution.py:24
  142.4 5.1 %collective-permute-done.7 = bf16[32,1024]{1,0:T(8,128)(2,1)S(1)} collective-permute-done((bf16[32,1024]{1,0:T(8,128)(2,1)S(1)}, bf16[32,1024]{1,0:T(8,128)(2,1)S(1)}, u32[]{:S(2)}, u32[]{:S(2)}) %collective-permute-start.7) | collective-permute-done | bytes 65568 | tf_op jit(solution)/shard_map/ppermute | solution.py:24
  147.5 1.9 %collective-permute-start.8 = (bf16[64,1024]{1,0:T(8,128)(2,1)S(1)}, bf16[64,1024]{1,0:T(8,128)(2,1)S(1)}, u32[]{:S(2)}, u32[]{:S(2)}) collective-permute-start(bf16[64,1024]{1,0:T(8,128)(2,1)S(1)} %maximum_select_fusion.3), channel_id=1, source_target_pairs={{0,32},{32,0},{64,96},{96,64},{1,33},{33,1},{65,97},{97,65},{2,34}... | collective-permute-start | bytes 393224 | tf_op jit(solution)/shard_map/ppermute | solution.py:24
  150.0 3.9 %collective-permute-done.8 = bf16[64,1024]{1,0:T(8,128)(2,1)S(1)} collective-permute-done((bf16[64,1024]{1,0:T(8,128)(2,1)S(1)}, bf16[64,1024]{1,0:T(8,128)(2,1)S(1)}, u32[]{:S(2)}, u32[]{:S(2)}) %collective-permute-start.8) | collective-permute-done | bytes 131104 | tf_op jit(solution)/shard_map/ppermute | solution.py:24
  154.0 3.3 %collective-permute-start.9 = (bf16[128,1024]{1,0:T(8,128)(2,1)S(1)}, bf16[128,1024]{1,0:T(8,128)(2,1)S(1)}, u32[]{:S(2)}, u32[]{:S(2)}) collective-permute-start(bf16[128,1024]{1,0:T(8,128)(2,1)S(1)} %maximum_select_fusion.2), channel_id=1, source_target_pairs={{0,16},{16,0},{1,17},{17,1},{2,18},{18,2},{3,19},{19,3},{4,20},{20... | collective-permute-start | bytes 786440 | tf_op jit(solution)/shard_map/ppermute | solution.py:24
  157.3 2.5 %fusion.12 = f32[1,512]{1,0:T(1,128)S(1)} fusion(f32[1024,1]{0,1:T(1,128)S(1)} %bitcast.51, bf16[1024,512]{1,0:T(8,128)(2,1)} %all-gather.2.cloned.1.call-done), kind=kOutput, calls=%fused_computation.22 | convolution fusion | flops 7340032 | bytes 1054720 | tf_op jit(solution)/shard_map/dot_general | solution.py:106
  (100 shorter events, 23.4 us)
Async XLA Ops:
  7.2 70.2 %copy-start = (bf16[1024,512]{1,0:T(8,128)(2,1)S(1)}, bf16[1024,512]{1,0:T(8,128)(2,1)}, u32[]{:S(2)}) copy-start(bf16[1024,512]{1,0:T(8,128)(2,1)} %param.12) | copy-start | bytes 3145732
  7.2 40.2 %copy-start.2 = (bf16[2048,64]{0,1:T(8,128)(2,1)S(1)}, bf16[2048,64]{0,1:T(8,128)(2,1)}, u32[]{:S(2)}) copy-start(bf16[2048,64]{0,1:T(8,128)(2,1)} %param.10) | copy-start | bytes 786436
  7.2 150.1 %all-gather.2.cloned.1.call-start = ((), (), s32[]{:S(2)}) async-start(), calls=%async_computation | async-start | bytes 1114112 | tf_op jit(solution)/shard_map/all_gather | solution.py:57
  9.8 38.6 %copy-start.3 = (f32[2048]{0:T(1024)S(1)}, f32[2048]{0:T(1024)}, u32[]{:S(2)}) copy-start(f32[2048]{0:T(1024)} %param.11) | copy-start | bytes 24580
  66.7 12.2 %collective-permute-start.10 = (f32[640]{0:T(1024)S(1)}, f32[640]{0:T(1024)S(1)}, u32[]{:S(2)}, u32[]{:S(2)}) collective-permute-start(f32[640]{0:T(1024)S(1)} %dynamic_slice.83), channel_id=1, source_target_pairs={{0,16},{16,0},{1,17},{17,1},{2,18},{18,2},{3,19},{19,3},{4,20},{20... | collective-permute-start | bytes 7688 | tf_op jit(solution)/shard_map/ppermute | solution.py:24
  75.5 10.1 %collective-permute-start = (f32[128,1024]{1,0:T(8,128)S(1)}, f32[128,1024]{1,0:T(8,128)S(1)}, u32[]{:S(2)}, u32[]{:S(2)}) collective-permute-start(f32[128,1024]{1,0:T(8,128)S(1)} %constant_dynamic-slice_fusion.5), channel_id=1, source_target_pairs={{0,16},{16,0},{1,17},{17,1},{2,18},{18,2},{3,19},{19,3},{4,20},{20... | collective-permute-start | bytes 1572872 | tf_op jit(solution)/shard_map/ppermute | solution.py:24
  79.0 4.3 %collective-permute-start.11 = (f32[320]{0:T(512)S(1)}, f32[320]{0:T(512)S(1)}, u32[]{:S(2)}, u32[]{:S(2)}) collective-permute-start(f32[320]{0:T(512)S(1)} %dynamic_slice.85), channel_id=1, source_target_pairs={{0,32},{32,0},{64,96},{96,64},{1,33},{33,1},{65,97},{97,65},{2,34}... | collective-permute-start | bytes 3848 | tf_op jit(solution)/shard_map/ppermute | solution.py:24
  83.5 5.3 %collective-permute-start.12 = (f32[160]{0:T(256)S(1)}, f32[160]{0:T(256)S(1)}, u32[]{:S(2)}, u32[]{:S(2)}) collective-permute-start(f32[160]{0:T(256)S(1)} %dynamic_slice.87), channel_id=1, source_target_pairs={{0,128},{128,0},{256,384},{384,256},{1,129},{129,1},{257,385},{385... | collective-permute-start | bytes 1928 | tf_op jit(solution)/shard_map/ppermute | solution.py:24
  85.7 13.4 %collective-permute-start.1 = (f32[64,1024]{1,0:T(8,128)S(1)}, f32[64,1024]{1,0:T(8,128)S(1)}, u32[]{:S(2)}, u32[]{:S(2)}) collective-permute-start(f32[64,1024]{1,0:T(8,128)S(1)} %constant_dynamic-slice_fusion.4), channel_id=1, source_target_pairs={{0,32},{32,0},{64,96},{96,64},{1,33},{33,1},{65,97},{97,65},{2,34}... | collective-permute-start | bytes 786440 | tf_op jit(solution)/shard_map/ppermute | solution.py:24
  89.0 6.4 %collective-permute-start.13 = (f32[80]{0:T(128)S(1)}, f32[80]{0:T(128)S(1)}, u32[]{:S(2)}, u32[]{:S(2)}) collective-permute-start(f32[80]{0:T(128)S(1)} %dynamic_slice.89), channel_id=1, source_target_pairs={{0,64},{32,96},{64,0},{96,32},{1,65},{33,97},{65,1},{97,33},{2,66}... | collective-permute-start | bytes 968 | tf_op jit(solution)/shard_map/ppermute | solution.py:24
  95.6 5.7 %collective-permute-start.14 = (f32[40]{0:T(128)S(1)}, f32[40]{0:T(128)S(1)}, u32[]{:S(2)}, u32[]{:S(2)}) collective-permute-start(f32[40]{0:T(128)S(1)} %dynamic_slice.91), channel_id=1, source_target_pairs={{0,256},{128,384},{256,0},{384,128},{1,257},{129,385},{257,1},{385... | collective-permute-start | bytes 488 | tf_op jit(solution)/shard_map/ppermute | solution.py:24
  99.2 6.6 %collective-permute-start.2 = (f32[32,1024]{1,0:T(8,128)S(1)}, f32[32,1024]{1,0:T(8,128)S(1)}, u32[]{:S(2)}, u32[]{:S(2)}) collective-permute-start(f32[32,1024]{1,0:T(8,128)S(1)} %constant_dynamic-slice_fusion.3), channel_id=1, source_target_pairs={{0,128},{128,0},{256,384},{384,256},{1,129},{129,1},{257,385},{385... | collective-permute-start | bytes 393224 | tf_op jit(solution)/shard_map/ppermute | solution.py:24
  101.4 8.3 %collective-permute-start.15 = (f32[40]{0:T(128)S(1)}, f32[40]{0:T(128)S(1)}, u32[]{:S(2)}, u32[]{:S(2)}) collective-permute-start(f32[40]{0:T(128)S(1)} %dynamic-slice_add_fusion.7), channel_id=1, source_target_pairs={{0,256},{128,384},{256,0},{384,128},{1,257},{129,385},{257,1},{385... | collective-permute-start | bytes 488 | tf_op jit(solution)/shard_map/ppermute | solution.py:24
  105.9 6.9 %collective-permute-start.3 = (f32[16,1024]{1,0:T(8,128)S(1)}, f32[16,1024]{1,0:T(8,128)S(1)}, u32[]{:S(2)}, u32[]{:S(2)}) collective-permute-start(f32[16,1024]{1,0:T(8,128)S(1)} %constant_dynamic-slice_fusion.2), channel_id=1, source_target_pairs={{0,64},{32,96},{64,0},{96,32},{1,65},{33,97},{65,1},{97,33},{2,66}... | collective-permute-start | bytes 196616 | tf_op jit(solution)/shard_map/ppermute | solution.py:24
  109.8 5.8 %collective-permute-start.16 = (f32[80]{0:T(128)S(1)}, f32[80]{0:T(128)S(1)}, u32[]{:S(2)}, u32[]{:S(2)}) collective-permute-start(f32[80]{0:T(128)S(1)} %broadcast_select_fusion.2), channel_id=1, source_target_pairs={{0,64},{32,96},{64,0},{96,32},{1,65},{33,97},{65,1},{97,33},{2,66}... | collective-permute-start | bytes 968 | tf_op jit(solution)/shard_map/ppermute | solution.py:24
  112.8 5.8 %collective-permute-start.4 = (f32[8,1024]{1,0:T(8,128)S(1)}, f32[8,1024]{1,0:T(8,128)S(1)}, u32[]{:S(2)}, u32[]{:S(2)}) collective-permute-start(f32[8,1024]{1,0:T(8,128)S(1)} %constant_dynamic-slice_fusion.1), channel_id=1, source_target_pairs={{0,256},{128,384},{256,0},{384,128},{1,257},{129,385},{257,1},{385... | collective-permute-start | bytes 98312 | tf_op jit(solution)/shard_map/ppermute | solution.py:24
  115.7 6.1 %collective-permute-start.17 = (f32[160]{0:T(256)S(1)}, f32[160]{0:T(256)S(1)}, u32[]{:S(2)}, u32[]{:S(2)}) collective-permute-start(f32[160]{0:T(256)S(1)} %maximum_select_fusion.9), channel_id=1, source_target_pairs={{0,128},{128,0},{256,384},{384,256},{1,129},{129,1},{257,385},{385... | collective-permute-start | bytes 1928 | tf_op jit(solution)/shard_map/ppermute | solution.py:24
  118.7 5.5 %collective-permute-start.5 = (bf16[8,1024]{1,0:T(8,128)(2,1)S(1)}, bf16[8,1024]{1,0:T(8,128)(2,1)S(1)}, u32[]{:S(2)}, u32[]{:S(2)}) collective-permute-start(bf16[8,1024]{1,0:T(8,128)(2,1)S(1)} %add_convert_fusion), channel_id=1, source_target_pairs={{0,256},{128,384},{256,0},{384,128},{1,257},{129,385},{257,1},{385... | collective-permute-start | bytes 49160 | tf_op jit(solution)/shard_map/ppermute | solution.py:24
  121.9 6.6 %collective-permute-start.18 = (f32[320]{0:T(512)S(1)}, f32[320]{0:T(512)S(1)}, u32[]{:S(2)}, u32[]{:S(2)}) collective-permute-start(f32[320]{0:T(512)S(1)} %maximum_select_fusion.8), channel_id=1, source_target_pairs={{0,32},{32,0},{64,96},{96,64},{1,33},{33,1},{65,97},{97,65},{2,34}... | collective-permute-start | bytes 3848 | tf_op jit(solution)/shard_map/ppermute | solution.py:24
  124.2 14.9 %collective-permute-start.6 = (bf16[16,1024]{1,0:T(8,128)(2,1)S(1)}, bf16[16,1024]{1,0:T(8,128)(2,1)S(1)}, u32[]{:S(2)}, u32[]{:S(2)}) collective-permute-start(bf16[16,1024]{1,0:T(8,128)(2,1)S(1)} %maximum_select_fusion.5), channel_id=1, source_target_pairs={{0,64},{32,96},{64,0},{96,32},{1,65},{33,97},{65,1},{97,33},{2,66}... | collective-permute-start | bytes 98312 | tf_op jit(solution)/shard_map/ppermute | solution.py:24
  128.5 13.8 %collective-permute-start.19 = (f32[640]{0:T(1024)S(1)}, f32[640]{0:T(1024)S(1)}, u32[]{:S(2)}, u32[]{:S(2)}) collective-permute-start(f32[640]{0:T(1024)S(1)} %maximum_select_fusion.7), channel_id=1, source_target_pairs={{0,16},{16,0},{1,17},{17,1},{2,18},{18,2},{3,19},{19,3},{4,20},{20... | collective-permute-start | bytes 7688 | tf_op jit(solution)/shard_map/ppermute | solution.py:24
  139.2 8.3 %collective-permute-start.7 = (bf16[32,1024]{1,0:T(8,128)(2,1)S(1)}, bf16[32,1024]{1,0:T(8,128)(2,1)S(1)}, u32[]{:S(2)}, u32[]{:S(2)}) collective-permute-start(bf16[32,1024]{1,0:T(8,128)(2,1)S(1)} %maximum_select_fusion.4), channel_id=1, source_target_pairs={{0,128},{128,0},{256,384},{384,256},{1,129},{129,1},{257,385},{385... | collective-permute-start | bytes 196616 | tf_op jit(solution)/shard_map/ppermute | solution.py:24
  147.5 6.4 %collective-permute-start.8 = (bf16[64,1024]{1,0:T(8,128)(2,1)S(1)}, bf16[64,1024]{1,0:T(8,128)(2,1)S(1)}, u32[]{:S(2)}, u32[]{:S(2)}) collective-permute-start(bf16[64,1024]{1,0:T(8,128)(2,1)S(1)} %maximum_select_fusion.3), channel_id=1, source_target_pairs={{0,32},{32,0},{64,96},{96,64},{1,33},{33,1},{65,97},{97,65},{2,34}... | collective-permute-start | bytes 393224 | tf_op jit(solution)/shard_map/ppermute | solution.py:24
  154.0 6.5 %collective-permute-start.9 = (bf16[128,1024]{1,0:T(8,128)(2,1)S(1)}, bf16[128,1024]{1,0:T(8,128)(2,1)S(1)}, u32[]{:S(2)}, u32[]{:S(2)}) collective-permute-start(bf16[128,1024]{1,0:T(8,128)(2,1)S(1)} %maximum_select_fusion.2), channel_id=1, source_target_pairs={{0,16},{16,0},{1,17},{17,1},{2,18},{18,2},{3,19},{19,3},{4,20},{20... | collective-permute-start | bytes 786440 | tf_op jit(solution)/shard_map/ppermute | solution.py:24
  157.3 3.1 %copy-start.1 = (bf16[1024,512]{1,0:T(8,128)(2,1)S(1)}, bf16[1024,512]{1,0:T(8,128)(2,1)}, u32[]{:S(2)}) copy-start(bf16[1024,512]{1,0:T(8,128)(2,1)} %all-gather.2.cloned.1.call-done) | copy-start | bytes 3145732
Sparse Core Ops, SparseCore 0:
  78.9 74.1 all-gather.1

commit v2 on v1

--- a/solution.py
+++ b/solution.py
@@ -30,17 +30,19 @@
 
 
 def cell_sum(total, masses):
+    parts = 2 ** len(HALVING)
+    genes, panel = total.shape
+    packed = jnp.concatenate(
+        [total.reshape(parts, -1), masses.reshape(parts, -1)], axis=1
+    )
     for axis, bit in HALVING:
-        keep_t, send_t = _half(total, axis, bit)
-        keep_m, send_m = _half(masses, axis, bit)
-        got_t, got_m = _swap((send_t, send_m), axis, bit)
-        total, masses = keep_t + got_t, keep_m + got_m
-    reduced = total.astype(jnp.bfloat16)
+        keep, send = _half(packed, axis, bit)
+        packed = keep + _swap(send, axis, bit)
     for axis, bit in reversed(HALVING):
-        got_t, got_m = _swap((reduced, masses), axis, bit)
-        reduced = _join(reduced, got_t, axis, bit)
-        masses = _join(masses, got_m, axis, bit)
-    return reduced, masses
+        packed = _join(packed, _swap(packed, axis, bit), axis, bit)
+    cut = total.size // parts
+    reduced = packed[:, :cut].reshape(genes, panel).astype(jnp.bfloat16)
+    return reduced, packed[:, cut:].reshape(-1)
 
 
 def local(rna_counts, rna_embed, rna_potential, atac_counts, atac_embed, atac_potential, panel_ids):
@@ -49,12 +51,13 @@
     chosen_rows = jnp.take(atac_counts, local_ids, axis=0)
     chosen_embed = jnp.take(atac_embed, local_ids, axis=0)
     chosen_potential = jnp.take(atac_potential, local_ids, axis=0)
-    small = jnp.concatenate([chosen_embed, chosen_potential[:, None]], axis=1)
-    small = lax.all_gather(small, "y", axis=0, tiled=True)
-    small = lax.all_gather(small, "z_hi", axis=0, tiled=True)
-    panel_embed = small[:, :-1]
-    panel_float = small[:, -1].astype(jnp.float32)
-    panel_rows = lax.all_gather(chosen_rows, FEAT, axis=0, tiled=True)
+    width = chosen_rows.shape[1]
+    panel = jnp.concatenate([chosen_rows, chosen_embed, chosen_potential[:, None]], axis=1)
+    panel = lax.all_gather(panel, "y", axis=0, tiled=True)
+    panel = lax.all_gather(panel, "z_hi", axis=0, tiled=True)
+    panel_rows = panel[:, :width]
+    panel_embed = panel[:, width:-1]
+    panel_float = panel[:, -1].astype(jnp.float32)
     inverse = 1.0 / math.sqrt(rna_embed.shape[1])
     rows_here = rna_counts.shape[0]
     genes_here = rna_counts.shape[1]

time: 170 us -> 203 us (1.19)
  waiting for transfers between devices: 13.9 us -> 108 us
  starting transfers between devices: 73 us -> 37 us
  blocking collectives: 35.6 us -> 11.6 us
    all_gather x1, waiting for transfers between devices: 0.02 us -> 75.9 us  [local(): panel = lax.all_gather(panel, 'z_hi', axis=0, tiled=True)]
    ppermute x20 -> x10, starting transfers between devices: 72.9 us -> 37 us  [_swap(): return lax.ppermute(value, axis, [(i, i ^ bit) for i in range(SIZES[axis])])]
    all_gather x2 -> x1, blocking collectives: 35.6 us -> 11.6 us  [local(): panel = lax.all_gather(panel, 'y', axis=0, tiled=True)]
    ppermute x20 -> x10, waiting for transfers between devices: 13.9 us -> 32.6 us  [_swap(): return lax.ppermute(value, axis, [(i, i ^ bit) for i in range(SIZES[axis])])]
  transfers between devices with their start and end apart: 21 -> 11, of which waited for: 7 -> 11; matrix products, arithmetic and copies ran while one was open for 4% -> 1% of each run, Pallas kernels for 0% -> 0%
where the time goes in v2:
time: 203 us
  waiting for transfers between devices  108 us (53%)
  starting transfers between devices  37 us (18%)
  matrix products  20.1 us (10%)
  between operations  14.4 us (7%)
  blocking collectives  11.6 us (6%)
  local copies, waits for them, and re-layouts  6.64 us (3%)
  other arithmetic  4.21 us (2%)
    all_gather x1, waiting for transfers between devices, local(): panel = lax.all_gather(panel, 'z_hi', axis=0, tiled=True)  75.9 us
    ppermute x10, starting transfers between devices, _swap(): return lax.ppermute(value, axis, [(i, i ^ bit) for i in range(SIZES[axis])])  37 us
    ppermute x10, waiting for transfers between devices, _swap(): return lax.ppermute(value, axis, [(i, i ^ bit) for i in range(SIZES[axis])])  32.6 us
    all_gather x1, blocking collectives, local(): panel = lax.all_gather(panel, 'y', axis=0, tiled=True)  11.6 us
    dot_general x4, matrix products, advance(): lax.dot_general(block_embed, panel_embed, (((1,), (1,)), ((), ())), prefe...  6.69 us
    dot_general x4, matrix products, advance(): lax.dot_general(block_rows, coupling, (((0,), (0,)), ((), ())), preferred...  5.96 us
    dot_general x4, matrix products, advance(): jnp.dot(row_mass, squares, precision=lax.Precision.HIGHEST)  5.05 us
  transfers between devices with their start and end apart: 11, of which 11 were waited for; matrix products, arithmetic and copies ran while one was open for 1% of the time, Pallas kernels for 0%

profile of v2, /device:TPU:1, one launch (start us, length us, event | category | flops | bytes accessed | tf_op | source)
XLA Modules:
  0.0 202.6 jit_solution(16096123120832869306)
XLA Ops:
  11.7 11.6 %all_gather.6 = bf16[256,577]{1,0:T(8,128)(2,1)} all-gather(bf16[64,577]{1,0:T(8,128)(2,1)S(1)} %pad_maximum_fusion), channel_id=1, replica_groups=mesh['z_lo'=4,'x'=4,'core'=2,'z_hi'=4,'y'=4] {'y'}, dimensions={0}, use_global_device_ids=true | all-gather | bytes 369280 | tf_op jit(solution)/shard_map/all_gather | solution.py:56
  24.3 75.9 %all-gather.2.cloned.1.call-done = bf16[1024,577]{1,0:T(8,128)(2,1)} async-done(((bf16[256,577]{1,0:T(8,128)(2,1)}), bf16[1024,577]{1,0:T(8,128)(2,1)}) %all-gather.2.cloned.1.call-update) | async-done | bytes 1181712 | tf_op jit(solution)/shard_map/all_gather | solution.py:57
  102.4 18.1 %while.15 = (s32[]{:T(128)}, f32[256,1024]{1,0:T(8,128)S(1)}, f32[256]{0:T(256)S(1)}, f32[1024]{0:T(1024)S(1)}, bf16[4,512,256]{2,1,0:T(8,128)(2,1)}, /*index=5*...) while((s32[]{:T(128)}, f32[256,1024]{1,0:T(8,128)S(1)}, ...), condition=%wide.region_3.4_spmd.clone, body=%wide.region_0.3_spmd.clone.sunk | while | flops 341574656 | bytes 5017213 | solution.py:97
  102.4 1.7 convert_reduce_fusion.4
  104.1 1.5 convolution_add_fusion.2
  105.6 1.3 fusion.34
  106.9 1.7 convert_reduce_fusion.4
  108.6 1.5 convolution_add_fusion.2
  111.5 1.7 convert_reduce_fusion.4
  113.1 1.5 convolution_add_fusion.2
  116.0 1.7 convert_reduce_fusion.4
  117.7 1.5 convolution_add_fusion.2
  121.0 3.2 %collective-permute-start = (f32[16,8232]{1,0:T(8,128)S(1)}, f32[16,8232]{1,0:T(8,128)S(1)}, u32[]{:S(2)}, u32[]{:S(2)}) collective-permute-start(f32[16,8232]{1,0:T(8,128)S(1)} %constant_dynamic-slice_fusion.5), channel_id=1, source_target_pairs={{0,16},{16,0},{1,17},{17,1},{2,18},{18,2},{3,19},{19,3},{4,20},{20... | collective-permute-start | bytes 1580552 | tf_op jit(solution)/shard_map/ppermute | solution.py:24
  124.2 1.5 collective-permute-done
  125.8 3.2 %collective-permute-start.1 = (f32[8,8232]{1,0:T(8,128)S(1)}, f32[8,8232]{1,0:T(8,128)S(1)}, u32[]{:S(2)}, u32[]{:S(2)}) collective-permute-start(f32[8,8232]{1,0:T(8,128)S(1)} %constant_dynamic-slice_fusion.4), channel_id=1, source_target_pairs={{0,32},{32,0},{64,96},{96,64},{1,33},{33,1},{65,97},{97,65},{2,34}... | collective-permute-start | bytes 790280 | tf_op jit(solution)/shard_map/ppermute | solution.py:24
  129.0 6.3 %collective-permute-done.1 = f32[8,8232]{1,0:T(8,128)S(1)} collective-permute-done((f32[8,8232]{1,0:T(8,128)S(1)}, f32[8,8232]{1,0:T(8,128)S(1)}, u32[]{:S(2)}, u32[]{:S(2)}) %collective-permute-start.1) | collective-permute-done | bytes 263456 | tf_op jit(solution)/shard_map/ppermute | solution.py:24
  135.3 1.9 collective-permute-start.2
  137.3 3.8 %collective-permute-done.2 = f32[4,8232]{1,0:T(4,128)S(1)} collective-permute-done((f32[4,8232]{1,0:T(4,128)S(1)}, f32[4,8232]{1,0:T(4,128)S(1)}, u32[]{:S(2)}, u32[]{:S(2)}) %collective-permute-start.2) | collective-permute-done | bytes 131744 | tf_op jit(solution)/shard_map/ppermute | solution.py:24
  141.1 4.7 %collective-permute-start.3 = (f32[2,8232]{1,0:T(2,128)S(1)}, f32[2,8232]{1,0:T(2,128)S(1)}, u32[]{:S(2)}, u32[]{:S(2)}) collective-permute-start(f32[2,8232]{1,0:T(2,128)S(1)} %constant_dynamic-slice_fusion.2), channel_id=1, source_target_pairs={{0,64},{32,96},{64,0},{96,32},{1,65},{33,97},{65,1},{97,33},{2,66}... | collective-permute-start | bytes 197576 | tf_op jit(solution)/shard_map/ppermute | solution.py:24
  145.8 1.8 collective-permute-done.3
  147.8 1.9 collective-permute-start.4
  149.7 4.0 %collective-permute-done.4 = f32[1,8232]{1,0:T(1,128)S(1)} collective-permute-done((f32[1,8232]{1,0:T(1,128)S(1)}, f32[1,8232]{1,0:T(1,128)S(1)}, u32[]{:S(2)}, u32[]{:S(2)}) %collective-permute-start.4) | collective-permute-done | bytes 32960 | tf_op jit(solution)/shard_map/ppermute | solution.py:24
  153.7 1.9 collective-permute-start.5
  155.7 3.8 %collective-permute-done.5 = f32[1,8232]{1,0:T(1,128)S(1)} collective-permute-done((f32[1,8232]{1,0:T(1,128)S(1)}, f32[1,8232]{1,0:T(1,128)S(1)}, u32[]{:S(2)}, u32[]{:S(2)}) %collective-permute-start.5) | collective-permute-done | bytes 32960 | tf_op jit(solution)/shard_map/ppermute | solution.py:24
  159.5 4.7 %collective-permute-start.6 = (f32[2,8232]{1,0:T(2,128)S(1)}, f32[2,8232]{1,0:T(2,128)S(1)}, u32[]{:S(2)}, u32[]{:S(2)}) collective-permute-start(f32[2,8232]{1,0:T(2,128)S(1)} %maximum_select_fusion.4), channel_id=1, source_target_pairs={{0,64},{32,96},{64,0},{96,32},{1,65},{33,97},{65,1},{97,33},{2,66}... | collective-permute-start | bytes 197576 | tf_op jit(solution)/shard_map/ppermute | solution.py:24
  164.2 1.8 collective-permute-done.6
  166.2 1.9 collective-permute-start.7
  168.1 4.1 %collective-permute-done.7 = f32[4,8232]{1,0:T(4,128)S(1)} collective-permute-done((f32[4,8232]{1,0:T(4,128)S(1)}, f32[4,8232]{1,0:T(4,128)S(1)}, u32[]{:S(2)}, u32[]{:S(2)}) %collective-permute-start.7) | collective-permute-done | bytes 131744 | tf_op jit(solution)/shard_map/ppermute | solution.py:24
  172.3 3.2 %collective-permute-start.8 = (f32[8,8232]{1,0:T(8,128)S(1)}, f32[8,8232]{1,0:T(8,128)S(1)}, u32[]{:S(2)}, u32[]{:S(2)}) collective-permute-start(f32[8,8232]{1,0:T(8,128)S(1)} %maximum_select_fusion.2), channel_id=1, source_target_pairs={{0,32},{32,0},{64,96},{96,64},{1,33},{33,1},{65,97},{97,65},{2,34}... | collective-permute-start | bytes 790280 | tf_op jit(solution)/shard_map/ppermute | solution.py:24
  175.4 4.0 %collective-permute-done.8 = f32[8,8232]{1,0:T(8,128)S(1)} collective-permute-done((f32[8,8232]{1,0:T(8,128)S(1)}, f32[8,8232]{1,0:T(8,128)S(1)}, u32[]{:S(2)}, u32[]{:S(2)}) %collective-permute-start.8) | collective-permute-done | bytes 263456 | tf_op jit(solution)/shard_map/ppermute | solution.py:24
  179.5 10.4 %collective-permute-start.9 = (f32[16,8232]{1,0:T(8,128)S(1)}, f32[16,8232]{1,0:T(8,128)S(1)}, u32[]{:S(2)}, u32[]{:S(2)}) collective-permute-start(f32[16,8232]{1,0:T(8,128)S(1)} %maximum_select_fusion.1), channel_id=1, source_target_pairs={{0,16},{16,0},{1,17},{17,1},{2,18},{18,2},{3,19},{19,3},{4,20},{20... | collective-permute-start | bytes 1580552 | tf_op jit(solution)/shard_map/ppermute | solution.py:24
  189.9 1.5 collective-permute-done.9
  (74 shorter events, 17.1 us)
Async XLA Ops:
  7.2 2.6 %copy-start = (bf16[1024,512]{1,0:T(8,128)(2,1)S(1)}, bf16[1024,512]{1,0:T(8,128)(2,1)}, u32[]{:S(2)}) copy-start(bf16[1024,512]{1,0:T(8,128)(2,1)} %param.12) | copy-start | bytes 3145732
  7.2 3.5 %copy-start.1 = (bf16[1024]{0:T(1024)(128)(2,1)S(1)}, bf16[1024]{0:T(1024)(128)(2,1)}, u32[]{:S(2)}) copy-start(bf16[1024]{0:T(1024)(128)(2,1)} %param.14) | copy-start | bytes 6148
  7.2 93.0 %all-gather.2.cloned.1.call-start = ((), (), s32[]{:S(2)}) async-start(), calls=%async_computation | async-start | bytes 1638400 | tf_op jit(solution)/shard_map/all_gather | solution.py:57
  8.0 15.3 %copy-start.2 = (bf16[2048,64]{0,1:T(8,128)(2,1)S(1)}, bf16[2048,64]{0,1:T(8,128)(2,1)}, u32[]{:S(2)}) copy-start(bf16[2048,64]{0,1:T(8,128)(2,1)} %param.10) | copy-start | bytes 786436
  10.5 13.8 %copy-start.4 = (f32[2048]{0:T(1024)S(1)}, f32[2048]{0:T(1024)}, u32[]{:S(2)}) copy-start(f32[2048]{0:T(1024)} %param.11) | copy-start | bytes 24580
  121.0 4.7 %collective-permute-start = (f32[16,8232]{1,0:T(8,128)S(1)}, f32[16,8232]{1,0:T(8,128)S(1)}, u32[]{:S(2)}, u32[]{:S(2)}) collective-permute-start(f32[16,8232]{1,0:T(8,128)S(1)} %constant_dynamic-slice_fusion.5), channel_id=1, source_target_pairs={{0,16},{16,0},{1,17},{17,1},{2,18},{18,2},{3,19},{19,3},{4,20},{20... | collective-permute-start | bytes 1580552 | tf_op jit(solution)/shard_map/ppermute | solution.py:24
  125.8 9.5 %collective-permute-start.1 = (f32[8,8232]{1,0:T(8,128)S(1)}, f32[8,8232]{1,0:T(8,128)S(1)}, u32[]{:S(2)}, u32[]{:S(2)}) collective-permute-start(f32[8,8232]{1,0:T(8,128)S(1)} %constant_dynamic-slice_fusion.4), channel_id=1, source_target_pairs={{0,32},{32,0},{64,96},{96,64},{1,33},{33,1},{65,97},{97,65},{2,34}... | collective-permute-start | bytes 790280 | tf_op jit(solution)/shard_map/ppermute | solution.py:24
  135.3 5.7 %collective-permute-start.2 = (f32[4,8232]{1,0:T(4,128)S(1)}, f32[4,8232]{1,0:T(4,128)S(1)}, u32[]{:S(2)}, u32[]{:S(2)}) collective-permute-start(f32[4,8232]{1,0:T(4,128)S(1)} %constant_dynamic-slice_fusion.3), channel_id=1, source_target_pairs={{0,128},{128,0},{256,384},{384,256},{1,129},{129,1},{257,385},{385... | collective-permute-start | bytes 395144 | tf_op jit(solution)/shard_map/ppermute | solution.py:24
  141.1 6.5 %collective-permute-start.3 = (f32[2,8232]{1,0:T(2,128)S(1)}, f32[2,8232]{1,0:T(2,128)S(1)}, u32[]{:S(2)}, u32[]{:S(2)}) collective-permute-start(f32[2,8232]{1,0:T(2,128)S(1)} %constant_dynamic-slice_fusion.2), channel_id=1, source_target_pairs={{0,64},{32,96},{64,0},{96,32},{1,65},{33,97},{65,1},{97,33},{2,66}... | collective-permute-start | bytes 197576 | tf_op jit(solution)/shard_map/ppermute | solution.py:24
  147.8 5.9 %collective-permute-start.4 = (f32[1,8232]{1,0:T(1,128)S(1)}, f32[1,8232]{1,0:T(1,128)S(1)}, u32[]{:S(2)}, u32[]{:S(2)}) collective-permute-start(f32[1,8232]{1,0:T(1,128)S(1)} %constant_dynamic-slice_fusion.1), channel_id=1, source_target_pairs={{0,256},{128,384},{256,0},{384,128},{1,257},{129,385},{257,1},{385... | collective-permute-start | bytes 98792 | tf_op jit(solution)/shard_map/ppermute | solution.py:24
  153.7 5.7 %collective-permute-start.5 = (f32[1,8232]{1,0:T(1,128)S(1)}, f32[1,8232]{1,0:T(1,128)S(1)}, u32[]{:S(2)}, u32[]{:S(2)}) collective-permute-start(f32[1,8232]{1,0:T(1,128)S(1)} %dynamic-slice_add_fusion.4), channel_id=1, source_target_pairs={{0,256},{128,384},{256,0},{384,128},{1,257},{129,385},{257,1},{385... | collective-permute-start | bytes 98792 | tf_op jit(solution)/shard_map/ppermute | solution.py:24
  159.5 6.5 %collective-permute-start.6 = (f32[2,8232]{1,0:T(2,128)S(1)}, f32[2,8232]{1,0:T(2,128)S(1)}, u32[]{:S(2)}, u32[]{:S(2)}) collective-permute-start(f32[2,8232]{1,0:T(2,128)S(1)} %maximum_select_fusion.4), channel_id=1, source_target_pairs={{0,64},{32,96},{64,0},{96,32},{1,65},{33,97},{65,1},{97,33},{2,66}... | collective-permute-start | bytes 197576 | tf_op jit(solution)/shard_map/ppermute | solution.py:24
  166.2 6.0 %collective-permute-start.7 = (f32[4,8232]{1,0:T(4,128)S(1)}, f32[4,8232]{1,0:T(4,128)S(1)}, u32[]{:S(2)}, u32[]{:S(2)}) collective-permute-start(f32[4,8232]{1,0:T(4,128)S(1)} %maximum_select_fusion.3), channel_id=1, source_target_pairs={{0,128},{128,0},{256,384},{384,256},{1,129},{129,1},{257,385},{385... | collective-permute-start | bytes 395144 | tf_op jit(solution)/shard_map/ppermute | solution.py:24
  172.3 7.2 %collective-permute-start.8 = (f32[8,8232]{1,0:T(8,128)S(1)}, f32[8,8232]{1,0:T(8,128)S(1)}, u32[]{:S(2)}, u32[]{:S(2)}) collective-permute-start(f32[8,8232]{1,0:T(8,128)S(1)} %maximum_select_fusion.2), channel_id=1, source_target_pairs={{0,32},{32,0},{64,96},{96,64},{1,33},{33,1},{65,97},{97,65},{2,34}... | collective-permute-start | bytes 790280 | tf_op jit(solution)/shard_map/ppermute | solution.py:24
  179.5 12.0 %collective-permute-start.9 = (f32[16,8232]{1,0:T(8,128)S(1)}, f32[16,8232]{1,0:T(8,128)S(1)}, u32[]{:S(2)}, u32[]{:S(2)}) collective-permute-start(f32[16,8232]{1,0:T(8,128)S(1)} %maximum_select_fusion.1), channel_id=1, source_target_pairs={{0,16},{16,0},{1,17},{17,1},{2,18},{18,2},{3,19},{19,3},{4,20},{20... | collective-permute-start | bytes 1580552 | tf_op jit(solution)/shard_map/ppermute | solution.py:24
  191.5 1.3 copy-start.3
Sparse Core Ops, SparseCore 0:
  23.4 76.7 all-gather.1
